TPU v7x, 32 devices: a whole 2x2x4 slice. The times are simulated.
32 devices in a mesh: groups: 2 (over y), ctx: 16 (over z, x, core).
Axes of the slice: x: 2, y: 2, z: 4, core: 2. Of those that a mesh axis runs over, the one named last changes fastest.
Arguments:
- queries: bfloat16 [512, 5120], P(('groups', 'ctx')), parts along dimension 0, may hold values from -45 to 45
- keys: bfloat16 [49152, 1024], P(('groups', 'ctx')), parts along dimension 0, may hold values from -5 to 5
- values: bfloat16 [49152, 1024], P(('groups', 'ctx')), parts along dimension 0, may hold values from -10 to 10
- block_mask: int32 [16, 2, 192], P('groups', None, 'ctx'), parts along dimension 0, may hold values from 0 to 1, as said below
- out_weight: bfloat16 [5120, 5120], P('ctx'), may hold values from -0.078125 to 0.078125
Outputs:
- projected: bfloat16 [512, 5120], P(('groups', 'ctx')), parts along dimension 0
There are 2 independent parts, one for each index of `groups`. A program takes and returns all parts, laid end to end along the dimension named above; an argument that names none is the same for every part. Nothing has to cross between parts.
Inputs may be any that keep to these rules, and one draw needn't show every extreme that they name: `block_mask`: for every key head and query block at least one key block is 1; the share of 1s differs between spans of 1536 positions.
All inputs are finite; a program needn't handle non-finite values.
Results may differ from a plain program's by a relative error of at most 0.0055.
Values may be sent and summed in bfloat16 or wider, within the bound.
A program may use at most 128 MiB of HBM per device.

v0:
```python
import math

import jax
import jax.numpy as jnp
from jax import lax
from jax.sharding import PartitionSpec as P

HEAD_SIZE = 128


NEG = -1e30


def shards(queries, keys, values, block_mask, out_weight):
    whole = lax.all_gather(queries, "ctx", axis=0, tiled=True)
    qtok, width = whole.shape
    kdev = keys.shape[0]
    heads_kv, query_block_count, key_block_count = block_mask.shape
    head_dim = HEAD_SIZE
    query_group = width // head_dim // heads_kv
    scale = 1.0 / math.sqrt(head_dim)
    query_tensor = whole.reshape(qtok, heads_kv, query_group, head_dim)
    key_tensor = keys.reshape(kdev, heads_kv, head_dim)
    value_tensor = values.reshape(kdev, heads_kv, head_dim)

    def head_scores(head):
        q_h = lax.dynamic_index_in_dim(query_tensor, head, 1, keepdims=False)
        k_h = lax.dynamic_index_in_dim(key_tensor, head, 1, keepdims=False)
        scores = jnp.einsum("qge,ke->gqk", q_h, k_h, preferred_element_type=jnp.float32) * scale
        blocks = lax.dynamic_index_in_dim(block_mask, head, 0, keepdims=False)
        live = jnp.broadcast_to(
            blocks[:, None, :, None] > 0,
            (
                query_block_count,
                qtok // query_block_count,
                key_block_count,
                kdev // key_block_count,
            ),
        )
        return (scores, live.reshape(qtok, kdev))

    def max_step(head, maxima):
        scores, live = head_scores(head)
        local = jnp.max(jnp.where(live[None], scores, NEG), axis=2)
        return lax.dynamic_update_slice(maxima, local.T[:, None, :], (0, head, 0))

    maxima = lax.fori_loop(
        0, heads_kv, max_step, jnp.full((qtok, heads_kv, query_group), NEG, jnp.float32)
    )
    row_max = lax.pmax(maxima, "ctx")

    def sum_step(head, carry):
        numer, denom = carry
        scores, live = head_scores(head)
        top = lax.dynamic_index_in_dim(row_max, head, 1, keepdims=False).T[:, :, None]
        probs = jnp.where(live[None], jnp.exp(scores - top), 0.0).astype(jnp.bfloat16)
        total = jnp.sum(probs.astype(jnp.float32), axis=2)
        v_h = lax.dynamic_index_in_dim(value_tensor, head, 1, keepdims=False)
        weighted = jnp.einsum("gqk,ke->qge", probs, v_h, preferred_element_type=jnp.float32)
        numer = lax.dynamic_update_slice(
            numer, weighted.reshape(qtok, 1, query_group * head_dim), (0, head, 0)
        )
        denom = lax.dynamic_update_slice(denom, total.T[:, None, :], (0, head, 0))
        return (numer, denom)

    start_numer = jnp.zeros((qtok, heads_kv, query_group * head_dim), jnp.float32)
    start_denom = jnp.zeros((qtok, heads_kv, query_group), jnp.float32)
    numer, denom = lax.fori_loop(0, heads_kv, sum_step, (start_numer, start_denom))
    numer = numer.reshape(qtok, width)
    denom = denom.reshape(qtok, heads_kv * query_group)
    num_rows, den_rows = (
        lax.psum_scatter(numer, "ctx", scatter_dimension=0, tiled=True),
        lax.psum_scatter(denom, "ctx", scatter_dimension=0, tiled=True),
    )
    own_rows = num_rows.shape[0]
    attn_rows = (num_rows.reshape(own_rows, -1, head_dim) / den_rows[:, :, None]).reshape(
        own_rows, width
    )
    attn_cols = lax.all_to_all(
        attn_rows.astype(jnp.bfloat16), "ctx", split_axis=1, concat_axis=0, tiled=True
    )
    summed = lax.psum_scatter(
        jnp.dot(attn_cols, out_weight, preferred_element_type=jnp.float32),
        "ctx",
        scatter_dimension=0,
        tiled=True,
    )
    return summed.astype(jnp.bfloat16)


def solution(mesh):
    return jax.shard_map(
        shards,
        mesh=mesh,
        in_specs=(
            P(("groups", "ctx"), None),
            P(("groups", "ctx"), None),
            P(("groups", "ctx"), None),
            P("groups", None, "ctx"),
            P("ctx", None),
        ),
        out_specs=P(("groups", "ctx"), None),
        check_vma=False,
    )
```

profile of v0, /device:TPU:0, one launch (start us, length us, event | category | flops | bytes accessed | tf_op | source)
XLA Modules:
  0.0 496.8 jit_solution(2088119072019379952)
XLA Ops:
  7.3 4.9 copy.38
  12.2 4.7 copy.42
  16.9 4.7 copy.37
  21.6 34.0 %all-gather.2.cloned.1.call-done = bf16[256,5120]{1,0:T(8,128)(2,1)} async-done(((bf16[16,5120]{1,0:T(8,128)(2,1)}), bf16[256,5120]{1,0:T(8,128)(2,1)}) %all-gather.2.cloned.1.call-update) | async-done | bytes 2621456 | tf_op jit(solution)/shard_map/all_gather | solution.py:15
  55.6 4.4 copy.39
  60.0 4.3 copy.43
  64.3 53.1 %while.28 = (s32[]{:T(128)}, f32[256,8,5]{0,2,1:T(8,128)S(1)}, s32[8,2,12]{2,1,0:T(2,128)}, bf16[1536,8,128]{2,0,1:T(8,128)(2,1)}, bf16[256,8,5,128]{3,0,2,1:T(8,128)(2,1)}, /*index=5*/s32[]{:T(128)}) while((s32[]{:T(128)}, f32[256,8,5]{0,2,1:T(8,128)S(1)}, s32[8,2,12]{2,1,0:T(2,128)}, bf16[1536,8,128]{2,0,1:T(8,128)(2,1)}, ...), condition=%wide.region_2.3_spmd, body=%wide.region_0.2_spmd.sunk | while | flops 509213472 | bytes 3102949 | solution.py:47
  66.1 2.2 copy.63
  68.4 2.5 fusion.31
  71.8 0.9 copy.62
  72.8 2.2 copy.63
  75.0 2.5 fusion.31
  79.4 2.2 copy.63
  81.6 2.5 fusion.31
  85.1 0.9 copy.62
  86.1 2.2 copy.63
  88.3 2.5 fusion.31
  92.7 2.2 copy.63
  94.9 2.5 fusion.31
  98.4 0.9 copy.62
  99.3 2.2 copy.63
  101.5 2.5 fusion.31
  106.0 2.2 copy.63
  108.2 2.5 fusion.31
  111.7 0.9 copy.62
  112.6 2.2 copy.63
  114.8 2.5 fusion.31
  117.4 59.4 %pmax.7 = f32[256,8,5]{0,2,1:T(8,128)S(1)} all-reduce(f32[256,8,5]{0,2,1:T(8,128)S(1)} %get-tuple-element.239), channel_id=1, replica_groups=mesh['groups'=2,'ctx'=16] {'ctx'}, use_global_device_ids=true, to_apply=%region_3.4 | all-reduce | flops 10240 | bytes 81920 | tf_op jit(solution)/shard_map/pmax | solution.py:50
  176.8 80.6 %while.29 = (s32[]{:T(128)}, f32[256,8,640]{0,2,1:T(8,128)}, f32[256,8,5]{0,2,1:T(8,128)S(1)}, bf16[1536,8,128]{0,2,1:T(8,128)(2,1)}, s32[8,2,12]{2,1,0:T(2,128)...) while((s32[]{:T(128)}, f32[256,8,640]{0,2,1:T(8,128)}, ...), condition=%wide.region_6.7_spmd, body=%wide.region_4.6_spmd.sunk | while | flops 1018428160 | bytes 13341961 | solution.py:68
  178.7 2.2 copy.65
  180.9 3.4 convert_reduce_fusion.2
  184.3 1.7 fusion.34
  188.7 2.2 copy.65
  190.9 3.4 convert_reduce_fusion.2
  194.4 1.7 fusion.34
  198.8 2.2 copy.65
  201.0 3.4 convert_reduce_fusion.2
  204.5 1.7 fusion.34
  208.9 2.2 copy.65
  211.1 3.4 convert_reduce_fusion.2
  214.5 1.7 fusion.34
  218.0 0.9 copy.64
  219.0 2.2 copy.65
  221.2 3.4 convert_reduce_fusion.2
  224.6 1.7 fusion.34
  228.1 0.9 copy.64
  229.1 2.2 copy.65
  231.3 3.4 convert_reduce_fusion.2
  234.7 1.7 fusion.34
  239.1 2.2 copy.65
  241.3 3.4 convert_reduce_fusion.2
  244.8 1.7 fusion.34
  249.2 2.2 copy.65
  251.4 3.4 convert_reduce_fusion.2
  254.8 1.7 fusion.34
  258.3 6.0 %copy.44 = f32[256,5120]{1,0:T(8,128)} copy(f32[256,5120]{0,1:T(8,128)} %bitcast.123) | data formatting | bytes 10485760 | tf_op jit(solution)/shard_map/reshape | solution.py:69
  264.3 46.3 %reduce-scatter.10.cloned.1.call-done = f32[16,40]{1,0:T(8,128)} async-done(((f32[256,40]{1,0:T(8,128)}), f32[16,40]{1,0:T(8,128)}) %reduce-scatter.10.cloned.1.call-update) | async-done | bytes 2576 | tf_op jit(solution)/shard_map/reduce_scatter | solution.py:73
  310.7 81.4 %reduce-scatter.6.cloned.1.call-done = f32[16,5120]{1,0:T(8,128)} async-done(((f32[256,5120]{1,0:T(8,128)}), f32[16,5120]{1,0:T(8,128)}) %reduce-scatter.6.cloned.1.call-update) | async-done | bytes 327696 | tf_op jit(solution)/shard_map/reduce_scatter | solution.py:72
  392.9 1.7 fusion.18
  394.6 1.1 all_to_all.14
  395.7 12.4 %all_to_all.19 = bf16[16,16,320]{2,0,1:T(8,128)(2,1)S(1)} all-to-all(bf16[16,16,320]{2,0,1:T(8,128)(2,1)S(1)} %copy.46), channel_id=1, replica_groups=mesh['groups'=2,'ctx'=16] {'ctx'}, dimensions={1} | all-to-all | bytes 327680 | tf_op jit(solution)/shard_map/all_to_all | solution.py:79
  408.2 3.9 fusion.19
  412.1 76.6 %reduce-scatter.8.cloned.1.call-done = f32[16,5120]{1,0:T(8,128)} async-done(((f32[256,5120]{1,0:T(8,128)}), f32[16,5120]{1,0:T(8,128)}) %reduce-scatter.8.cloned.1.call-update) | async-done | bytes 327696 | tf_op jit(solution)/shard_map/reduce_scatter | solution.py:82
  488.6 1.7 convert_element_type.21
  (91 shorter events, 33.5 us)
Async XLA Ops:
  6.5 401.6 %copy-start = (bf16[320,5120]{1,0:T(8,128)(2,1)S(1)}, bf16[320,5120]{1,0:T(8,128)(2,1)}, u32[]{:S(2)}) copy-start(bf16[320,5120]{1,0:T(8,128)(2,1)} %param.13) | copy-start | bytes 9830404
  6.5 49.0 %all-gather.2.cloned.1.call-start = ((), (), s32[]{:S(2)}) async-start(), calls=%async_computation.4 | async-start | bytes 2785280 | tf_op jit(solution)/shard_map/all_gather | solution.py:15
  7.3 303.4 %reduce-scatter.10.cloned.1.call-start = ((), (), s32[]{:S(2)}) async-start(), calls=%async_computation.7 | async-start | bytes 139264 | tf_op jit(solution)/shard_map/reduce_scatter | solution.py:73
  258.2 133.8 %reduce-scatter.6.cloned.1.call-start = ((), (), s32[]{:S(2)}) async-start(), calls=%async_computation.5 | async-start | bytes 5570560 | tf_op jit(solution)/shard_map/reduce_scatter | solution.py:72
  264.3 224.4 %reduce-scatter.8.cloned.1.call-start = ((), (), s32[]{:S(2)}) async-start(), calls=%async_computation.6 | async-start | bytes 5570560 | tf_op jit(solution)/shard_map/reduce_scatter | solution.py:82
Sparse Core Ops, SparseCore 0:
  9.6 45.8 all-gather.1
  258.4 52.2 reduce-scatter.9
  314.5 77.4 reduce-scatter.5
  412.2 76.4 reduce-scatter.7
where the time goes:
time: 499 us; the launch traced here: 497 us
  waiting for transfers between devices  239 us (48%)
  local copies, waits for them, and re-layouts  92.9 us (19%)
  blocking collectives  71.9 us (14%)
  matrix products  64.9 us (13%)
  other arithmetic  14.3 us (3%)
  between operations  13.2 us (3%)
    reduce_scatter x1, waiting for transfers between devices, shards(): lax.psum_scatter(numer, 'ctx', scatter_dimension=0, tiled=True)  81.4 us
    reduce_scatter x1, waiting for transfers between devices, shards(): lax.psum_scatter(jnp.dot(attn_cols, out_weight, preferred_element_type=jn...  76.6 us
    pmax x1, blocking collectives, shards(): row_max = lax.pmax(maxima, 'ctx')  59.4 us
    dot_general x16, matrix products, head_scores(): jnp.einsum('qge,ke->gqk', q_h, k_h, preferred_element_type=jnp.float32)  47.6 us
    reduce_scatter x1, waiting for transfers between devices, shards(): lax.psum_scatter(denom, 'ctx', scatter_dimension=0, tiled=True)  46.3 us
    all_gather x1, waiting for transfers between devices, shards(): whole = lax.all_gather(queries, 'ctx', axis=0, tiled=True)  34 us
    broadcast_in_dim x8, local copies, waits for them, and re-layouts, max_step(): local = jnp.max(jnp.where(live[None], scores, NEG), axis=2)  17.8 us
    broadcast_in_dim x8, local copies, waits for them, and re-layouts, sum_step(): jnp.where(live[None], jnp.exp(scores - top), 0.0).astype(jnp.bfloat16)  17.8 us
  transfers between devices with their start and end apart: 4, of which 4 were waited for; matrix products, arithmetic and copies ran while one was open for 4% of the time, Pallas kernels for 0%

commit v1 on v0

v1 whole, which is shorter than its diff:
```python
import functools
import math

import jax
import jax.numpy as jnp
from jax import lax
from jax.experimental import pallas as pl
from jax.experimental.pallas import tpu as pltpu
from jax.sharding import PartitionSpec as P

HEAD_SIZE = 128
NEG = -1e30
LOG2E = math.log2(math.e)
MESH = pl.DeviceIdType.MESH


def attend_kernel(mask_ref, q_ref, k_ref, v_ref, numer_ref, top_ref, total_ref, live_ref, score_ref):
    head = pl.program_id(0)
    query_blocks, key_blocks = mask_ref.shape[1:]
    key_block = k_ref.shape[0] // key_blocks
    query_block = q_ref.shape[0] // query_blocks
    group = q_ref.shape[1] // HEAD_SIZE
    factor = LOG2E / math.sqrt(HEAD_SIZE)
    for at in range(query_blocks):
        rows = pl.ds(at * query_block, query_block)
        count = jnp.int32(0)
        for block in range(key_blocks):
            live_ref[count] = block
            count = count + (mask_ref[head, at, block] > 0).astype(jnp.int32)
        live_ref[count] = 0
        stacked = jnp.concatenate(
            [q_ref[rows, g * HEAD_SIZE : (g + 1) * HEAD_SIZE] for g in range(group)], axis=0
        )
        lanes = stacked.shape[0]
        pairs = (count + 1) // 2

        def block_of(ref, which):
            start = pl.multiple_of(live_ref[which] * key_block, key_block)
            return ref[pl.ds(start, key_block), :]

        def score_step(pair, top):
            both = jnp.concatenate([block_of(k_ref, 2 * pair), block_of(k_ref, 2 * pair + 1)], axis=0)
            scores = lax.dot_general(
                both, stacked, (((1,), (1,)), ((), ())), preferred_element_type=jnp.float32
            ) * factor
            score_ref[pair] = scores
            half = jnp.max(scores[:key_block].reshape(key_block // 8, 8, lanes), axis=0)
            other = jnp.max(scores[key_block:].reshape(key_block // 8, 8, lanes), axis=0)
            other = jnp.where(2 * pair + 1 < count, other, NEG)
            return jnp.maximum(top, jnp.maximum(half, other))

        top = lax.fori_loop(0, pairs, score_step, jnp.full((8, lanes), NEG, jnp.float32))
        top = jnp.max(top, axis=0, keepdims=True)

        def sum_step(pair, carry):
            numer, total = carry
            probs = jnp.exp2(score_ref[pair] - top)
            upper = jnp.where(2 * pair + 1 < count, probs[key_block:], 0.0)
            probs = jnp.concatenate([probs[:key_block], upper], axis=0).astype(jnp.bfloat16)
            total = total + jnp.sum(
                probs.astype(jnp.float32).reshape(2 * key_block // 8, 8, lanes), axis=0
            )
            both = jnp.concatenate([block_of(v_ref, 2 * pair), block_of(v_ref, 2 * pair + 1)], axis=0)
            numer = numer + lax.dot_general(
                both, probs, (((0,), (0,)), ((), ())), preferred_element_type=jnp.float32
            )
            return numer, total

        numer, total = lax.fori_loop(
            0,
            pairs,
            sum_step,
            (jnp.zeros((HEAD_SIZE, lanes), jnp.float32), jnp.zeros((8, lanes), jnp.float32)),
        )
        top_ref[0, at : at + 1, :] = top
        total_ref[0, at : at + 1, :] = jnp.sum(total, axis=0, keepdims=True)
        for g in range(group):
            columns = slice(g * query_block, (g + 1) * query_block)
            numer_ref[rows, g * HEAD_SIZE : (g + 1) * HEAD_SIZE] = numer[:, columns].T.astype(
                numer_ref.dtype
            )


def attend(whole, keys, values, block_mask, numer_type):
    qtok, width = whole.shape
    kdev = keys.shape[0]
    heads_kv, query_blocks, key_blocks = block_mask.shape
    columns = width // heads_kv
    lanes = columns // HEAD_SIZE * (qtok // query_blocks)
    stat = jax.ShapeDtypeStruct((heads_kv, query_blocks, lanes), jnp.float32)
    stat_spec = pl.BlockSpec((1, query_blocks, lanes), lambda h: (h, 0, 0))
    return pl.pallas_call(
        attend_kernel,
        grid=(heads_kv,),
        out_shape=(jax.ShapeDtypeStruct((qtok, width), numer_type), stat, stat),
        in_specs=[
            pl.BlockSpec(memory_space=pltpu.SMEM),
            pl.BlockSpec((qtok, columns), lambda h: (0, h)),
            pl.BlockSpec((kdev, HEAD_SIZE), lambda h: (0, h)),
            pl.BlockSpec((kdev, HEAD_SIZE), lambda h: (0, h)),
        ],
        out_specs=(pl.BlockSpec((qtok, columns), lambda h: (0, h)), stat_spec, stat_spec),
        scratch_shapes=[
            pltpu.SMEM((key_blocks + 2,), jnp.int32),
            pltpu.VMEM(((key_blocks + 1) // 2, 2 * kdev // key_blocks, lanes), jnp.float32),
        ],
        compiler_params=pltpu.CompilerParams(vmem_limit_bytes=40 * 2**20),
        name="attend",
    )(block_mask, whole, keys, values)


def by_token(stat, qtok):
    heads_kv, query_blocks, _ = stat.shape
    stat = stat.reshape(heads_kv, query_blocks, -1, qtok // query_blocks)
    return stat.transpose(1, 3, 0, 2).reshape(qtok, -1)


def shards_any(queries, keys, values, block_mask, out_weight):
    whole = lax.all_gather(queries, "ctx", axis=0, tiled=True)
    qtok, width = whole.shape
    numer, top, total = attend(whole, keys, values, block_mask, jnp.float32)
    rescale = by_token(jnp.exp2(top - lax.pmax(top, "ctx")), qtok)
    denom = by_token(total, qtok) * rescale
    numer = (numer.reshape(qtok, -1, HEAD_SIZE) * rescale[:, :, None]).reshape(qtok, width)
    num_rows = lax.psum_scatter(numer, "ctx", scatter_dimension=0, tiled=True)
    den_rows = lax.psum_scatter(denom, "ctx", scatter_dimension=0, tiled=True)
    own_rows = num_rows.shape[0]
    attn_rows = (num_rows.reshape(own_rows, -1, HEAD_SIZE) / den_rows[:, :, None]).reshape(
        own_rows, width
    )
    attn_cols = lax.all_to_all(
        attn_rows.astype(jnp.bfloat16), "ctx", split_axis=1, concat_axis=0, tiled=True
    )
    summed = lax.psum_scatter(
        jnp.dot(attn_cols, out_weight, preferred_element_type=jnp.float32),
        "ctx",
        scatter_dimension=0,
        tiled=True,
    )
    return summed.astype(jnp.bfloat16)


def solution(mesh):
    return jax.shard_map(
        shards_any,
        mesh=mesh,
        in_specs=(
            P(("groups", "ctx"), None),
            P(("groups", "ctx"), None),
            P(("groups", "ctx"), None),
            P("groups", None, "ctx"),
            P("ctx", None),
        ),
        out_specs=P(("groups", "ctx"), None),
        check_vma=False,
    )
```

time: 499 us -> 400 us (0.80)
  local copies, waits for them, and re-layouts: 92.9 us -> 15.3 us
  matrix products: 64.9 us -> 3.86 us
  Pallas kernels: 0 us -> 31.4 us
  waiting for transfers between devices: 239 us -> 252 us
  other arithmetic: 14.3 us -> 7.18 us
  blocking collectives: 71.9 us -> 77.4 us
    dot_general x25 -> x1, matrix products: 64.9 us -> 3.86 us  [shards_any(): jnp.dot(attn_cols, out_weight, preferred_element_type=jnp.float32)]
    broadcast_in_dim x32 -> x0, local copies, waits for them, and re-layouts: 38.8 us -> none  [the longest x8 17.8 us: max_step(): local = jnp.max(jnp.where(live[None], scores, NEG), axis=2)]
    pallas_call x0 -> x1, Pallas kernels: none -> 31.4 us  [attend(): pl.pallas_call(attend_kernel, grid=(heads_kv,), out_shape=(jax.ShapeDtype...]
    while x18 -> x0, local copies, waits for them, and re-layouts: 24.1 us -> none
    all_gather x1, waiting for transfers between devices: 34 us -> 48.3 us  [shards_any(): whole = lax.all_gather(queries, 'ctx', axis=0, tiled=True)]
    gt x16 -> x0, other arithmetic: 11 us -> none  [head_scores(): blocks[:, None, :, None] > 0]
    dynamic_update_slice x24 -> x0, local copies, waits for them, and re-layouts: 7.29 us -> none  [the longest x8 7.16 us: sum_step(): lax.dynamic_update_slice(numer, weighted.reshape(qtok, 1, query_group * h...]
    pmax x1, blocking collectives: 59.4 us -> 65 us  [shards_any(): rescale = by_token(jnp.exp2(top - lax.pmax(top, 'ctx')), qtok)]
  transfers between devices with their start and end apart: 4 -> 4, of which waited for: 4 -> 4; matrix products, arithmetic and copies ran while one was open for 4% -> 1% of each run, Pallas kernels for 0% -> 0%
where the time goes in v1:
time: 400 us
  waiting for transfers between devices  252 us (63%)
  blocking collectives  77.4 us (19%)
  Pallas kernels  31.4 us (8%)
  local copies, waits for them, and re-layouts  15.3 us (4%)
  between operations  13.2 us (3%)
  other arithmetic  7.18 us (2%)
    reduce_scatter x1, waiting for transfers between devices, shards_any(): num_rows = lax.psum_scatter(numer, 'ctx', scatter_dimension=0, tiled=True)  81.4 us
    reduce_scatter x1, waiting for transfers between devices, shards_any(): lax.psum_scatter(jnp.dot(attn_cols, out_weight, preferred_element_type=jn...  76.5 us
    pmax x1, blocking collectives, shards_any(): rescale = by_token(jnp.exp2(top - lax.pmax(top, 'ctx')), qtok)  65 us
    all_gather x1, waiting for transfers between devices, shards_any(): whole = lax.all_gather(queries, 'ctx', axis=0, tiled=True)  48.3 us
    reduce_scatter x1, waiting for transfers between devices, shards_any(): den_rows = lax.psum_scatter(denom, 'ctx', scatter_dimension=0, tiled=True)  44.7 us
    pallas_call x1, Pallas kernels, attend(): pl.pallas_call(attend_kernel, grid=(heads_kv,), out_shape=(jax.ShapeDtype...  31.4 us
    all_to_all x1, blocking collectives, shards_any(): lax.all_to_all(attn_rows.astype(jnp.bfloat16), 'ctx', split_axis=1, conca...  12.4 us
    unnamed x16, local copies, waits for them, and re-layouts  10.3 us
  transfers between devices with their start and end apart: 4, of which 4 were waited for; matrix products, arithmetic and copies ran while one was open for 1% of the time, Pallas kernels for 0%

profile of v1, /device:TPU:0, one launch (start us, length us, event | category | flops | bytes accessed | tf_op | source)
XLA Modules:
  0.0 400.1 jit_solution(15124819001877959116)
XLA Ops:
  6.5 0.0 copy-start
  6.5 0.0 all-gather.2.cloned.1.call-start
  6.5 0.7 all-gather.2.cloned.1.call-update
  7.3 0.0 reduce-scatter.10.cloned.1.call-start
  7.3 48.3 %all-gather.2.cloned.1.call-done.q_ref = bf16[256,5120]{1,0:T(8,128)(2,1)} async-done(((bf16[16,5120]{1,0:T(8,128)(2,1)}), bf16[256,5120]{1,0:T(8,128)(2,1)}) %all-gather.2.cloned.1.call-update) | async-done | bytes 2621456 | tf_op jit(solution)/shard_map/all_gather | solution.py:119
  55.6 0.0 copy-start.3
  55.6 1.9 copy-done.3
  57.5 0.0 copy-start.4
  57.5 1.9 copy-done.4
  59.4 0.0 copy-start.5
  59.4 1.7 copy-done.5
  61.1 0.0 copy-start.6
  61.1 0.7 copy-done.6
  61.8 31.4 %attend.1 = (f32[256,5120]{1,0:T(8,128)S(1)}, f32[8,2,640]{2,1,0:T(2,128)S(1)}, f32[8,2,640]{2,1,0:T(2,128)S(1)}) custom-call(s32[8,2,12]{2,1,0:T(2,128)S(1)} %copy-done.6, bf16[256,5120]{1,0:T(8,128)(2,1)S(1)} %copy-done.5, bf16[1536,1024]{1,0:T(8,128)(2,1)S(1)} %copy-done.3, bf16[1536,1024]{1,0:T(8,128)(2,1)S(1)} %copy-done.4), custom_call_target="tpu_custom_call" | custom-call | tf_op jit(solution)/shard_map/attend/pallas_call | solution.py:92
  93.2 0.0 copy-start.1
  93.2 2.3 copy-done.1
  95.5 65.0 %pmax.7 = f32[8,2,640]{2,1,0:T(2,128)S(1)} all-reduce(f32[8,2,640]{2,1,0:T(2,128)S(1)} %get-tuple-element.9), channel_id=1, replica_groups=mesh['groups'=2,'ctx'=16] {'ctx'}, use_global_device_ids=true, to_apply=%region_0.0 | all-reduce | flops 10240 | bytes 81920 | tf_op jit(solution)/shard_map/pmax | solution.py:122
  160.6 0.1 copy.15
  160.7 0.6 copy.16
  161.3 0.8 reshape.22
  162.1 0.8 copy.20
  162.9 0.0 reduce-scatter.10.cloned.1.call-update
  162.9 0.0 reduce-scatter.6.cloned.1.call-start
  163.0 0.0 copy-start.2
  163.0 1.5 mul.17
  164.5 1.0 copy-done.2
  165.5 3.8 bitcast_multiply_fusion
  169.2 0.0 reduce-scatter.6.cloned.1.call-update
  169.3 0.0 reduce-scatter.8.cloned.1.call-start
  169.3 44.7 %reduce-scatter.10.cloned.1.call-done = f32[16,40]{1,0:T(8,128)} async-done(((f32[256,40]{1,0:T(8,128)}), f32[16,40]{1,0:T(8,128)}) %reduce-scatter.10.cloned.1.call-update) | async-done | bytes 2576 | tf_op jit(solution)/shard_map/reduce_scatter | solution.py:126
  214.0 81.4 %reduce-scatter.6.cloned.1.call-done = f32[16,5120]{1,0:T(8,128)} async-done(((f32[256,5120]{1,0:T(8,128)}), f32[16,5120]{1,0:T(8,128)}) %reduce-scatter.6.cloned.1.call-update) | async-done | bytes 327696 | tf_op jit(solution)/shard_map/reduce_scatter | solution.py:125
  295.4 0.8 div.11
  296.2 1.7 fusion
  297.9 1.1 all_to_all.14
  299.1 12.4 %all_to_all.19 = bf16[16,16,320]{2,0,1:T(8,128)(2,1)S(1)} all-to-all(bf16[16,16,320]{2,0,1:T(8,128)(2,1)S(1)} %copy.19), channel_id=1, replica_groups=mesh['groups'=2,'ctx'=16] {'ctx'}, dimensions={1} | all-to-all | bytes 327680 | tf_op jit(solution)/shard_map/all_to_all | solution.py:131
  311.5 0.0 copy-done
  311.5 3.9 fusion.1
  315.4 0.0 reduce-scatter.8.cloned.1.call-update
  315.4 76.5 %reduce-scatter.8.cloned.1.call-done = f32[16,5120]{1,0:T(8,128)} async-done(((f32[256,5120]{1,0:T(8,128)}), f32[16,5120]{1,0:T(8,128)}) %reduce-scatter.8.cloned.1.call-update) | async-done | bytes 327696 | tf_op jit(solution)/shard_map/reduce_scatter | solution.py:134
  391.9 1.7 convert_element_type.7
  (8 shorter events, 0.2 us)
Async XLA Ops:
  6.5 305.0 %copy-start = (bf16[320,5120]{1,0:T(8,128)(2,1)S(1)}, bf16[320,5120]{1,0:T(8,128)(2,1)}, u32[]{:S(2)}) copy-start(bf16[320,5120]{1,0:T(8,128)(2,1)} %param.9) | copy-start | bytes 9830404
  6.5 49.0 %all-gather.2.cloned.1.call-start = ((), (), s32[]{:S(2)}) async-start(), calls=%async_computation.4 | async-start | bytes 2785280 | tf_op jit(solution)/shard_map/all_gather | solution.py:119
  7.3 206.8 %reduce-scatter.10.cloned.1.call-start = ((), (), s32[]{:S(2)}) async-start(), calls=%async_computation.7 | async-start | bytes 139264 | tf_op jit(solution)/shard_map/reduce_scatter | solution.py:126
  55.6 1.9 copy-start.3
  57.5 1.9 copy-start.4
  59.4 1.7 copy-start.5
  61.1 0.7 copy-start.6
  93.2 2.3 copy-start.1
  162.9 132.4 %reduce-scatter.6.cloned.1.call-start = ((), (), s32[]{:S(2)}) async-start(), calls=%async_computation.5 | async-start | bytes 5570560 | tf_op jit(solution)/shard_map/reduce_scatter | solution.py:125
  163.0 2.5 copy-start.2
  169.3 222.7 %reduce-scatter.8.cloned.1.call-start = ((), (), s32[]{:S(2)}) async-start(), calls=%async_computation.6 | async-start | bytes 5570560 | tf_op jit(solution)/shard_map/reduce_scatter | solution.py:134
Sparse Core Ops, SparseCore 0:
  9.6 45.8 all-gather.1
  163.0 50.9 reduce-scatter.9
  217.9 77.4 reduce-scatter.5
  315.5 76.3 reduce-scatter.7

commit v2 on v1

--- a/solution.py
+++ b/solution.py
@@ -140,9 +140,366 @@
     return summed.astype(jnp.bfloat16)
 
 
+CORES, ROW = 2, 2
+
+
+def place(n):
+    me = lax.axis_index("ctx")
+    core = lax.rem(me, CORES)
+    x = lax.rem(me // CORES, ROW)
+    plane = me // (CORES * ROW)
+    return me, plane, x, core
+
+
+def index_of(plane, x, core):
+    return (plane * ROW + x) * CORES + core
+
+
+def greet(devices):
+    barrier = pltpu.get_barrier_semaphore()
+    for device in devices:
+        pl.semaphore_signal(barrier, inc=1, device_id={"ctx": device}, device_id_type=MESH)
+    pl.semaphore_wait(barrier, len(devices))
+
+
+def remote(src, dst, send, recv, device):
+    return pltpu.make_async_remote_copy(
+        src_ref=src,
+        dst_ref=dst,
+        send_sem=send,
+        recv_sem=recv,
+        device_id={"ctx": device},
+        device_id_type=MESH,
+    )
+
+
+def gather_kernel(n, own_ref, whole_ref, own_sem, send_sem, recv_sem):
+    me, plane, x, core = place(n)
+    planes = n // (CORES * ROW)
+    beside, sibling = 1 - x, 1 - core
+    across = [lax.rem(plane + step, planes) for step in range(1, planes)]
+    greet(
+        [index_of(p, x, core) for p in across]
+        + [index_of(plane, beside, core), index_of(plane, x, sibling)]
+    )
+    own = pltpu.make_async_copy(own_ref, whole_ref.at[me], own_sem)
+    own.start()
+    sends = []
+
+    def send(src, block, slot, device):
+        copy = remote(src, whole_ref.at[block], send_sem.at[slot], recv_sem.at[block], device)
+        copy.start()
+        sends.append(copy)
+
+    def arrived(block, device):
+        remote(own_ref, whole_ref.at[block], send_sem.at[0], recv_sem.at[block], device).wait_recv()
+
+    slot = 0
+    for p in across:
+        send(own_ref, me, slot, index_of(p, x, core))
+        slot += 1
+    send(own_ref, me, slot, index_of(plane, beside, core))
+    send(own_ref, me, slot + 1, index_of(plane, x, sibling))
+    slot += 2
+    for step in range(planes):
+        if step:
+            block = index_of(lax.rem(plane + planes - step, planes), x, core)
+            arrived(block, me)
+            send(whole_ref.at[block], block, slot, index_of(plane, beside, core))
+            send(whole_ref.at[block], block, slot + 1, index_of(plane, x, sibling))
+            slot += 2
+    for step in range(planes):
+        block = index_of(lax.rem(plane + planes - step, planes), beside, core)
+        arrived(block, me)
+        send(whole_ref.at[block], block, slot, index_of(plane, x, sibling))
+        slot += 1
+    for step in range(planes):
+        for side in (x, beside):
+            arrived(index_of(lax.rem(plane + planes - step, planes), side, sibling), me)
+    for copy in sends:
+        copy.wait_send()
+    own.wait()
+
+
+def gather_rows(queries, n):
+    rows, width = queries.shape
+    whole = pl.pallas_call(
+        functools.partial(gather_kernel, n),
+        out_shape=jax.ShapeDtypeStruct((n, rows, width), queries.dtype),
+        in_specs=[pl.BlockSpec(memory_space=pltpu.VMEM)],
+        out_specs=pl.BlockSpec(memory_space=pltpu.VMEM),
+        scratch_shapes=[
+            pltpu.SemaphoreType.DMA,
+            pltpu.SemaphoreType.DMA((n,)),
+            pltpu.SemaphoreType.DMA((n,)),
+        ],
+        compiler_params=pltpu.CompilerParams(collective_id=0, has_side_effects=True),
+        name="gather_rows",
+    )(queries)
+    return whole.reshape(n * rows, width)
+
+
+def reduce_rows(place_of, parts, merge, finish):
+    plane, x, core, planes = place_of
+    beside, sibling = 1 - x, 1 - core
+    order = [lax.rem(plane + step, planes) for step in range(1, planes)] + [plane]
+
+    def core_copy(part, p):
+        src, got, _, _, _, _, sem = part
+        return remote(
+            src.at[p, :, sibling], got.at[p], sem.at[0, p], sem.at[1, p], index_of(plane, x, sibling)
+        )
+
+    def beside_copy(part, p):
+        _, _, held, got, _, _, sem = part
+        return remote(
+            held.at[p, beside], got.at[p], sem.at[2, p], sem.at[3, p], index_of(plane, beside, core)
+        )
+
+    def plane_copy(part, p, slot):
+        _, _, _, _, summed, got, sem = part
+        return remote(summed.at[p], got.at[slot], sem.at[4, p], sem.at[5, slot], index_of(p, x, core))
+
+    for p in order:
+        for part in parts:
+            core_copy(part, p).start()
+
+    def turn(step):
+        return lax.rem(plane + 1 + step, planes)
+
+    def from_core(step, _):
+        p = turn(step)
+        for part in parts:
+            core_copy(part, p).wait_recv()
+        for side in range(ROW):
+            merge(
+                [part[0].at[p, side, core] for part in parts],
+                [part[1].at[p, side] for part in parts],
+                [part[2].at[p, side] for part in parts],
+            )
+        for part in parts:
+            beside_copy(part, p).start()
+        return 0
+
+    lax.fori_loop(0, planes, from_core, 0)
+
+    def from_beside(step, _):
+        p = turn(step)
+        for part in parts:
+            beside_copy(part, p).wait_recv()
+        merge(
+            [part[2].at[p, x] for part in parts],
+            [part[3].at[p] for part in parts],
+            [part[4].at[p] for part in parts],
+        )
+
+        @pl.when(step < planes - 1)
+        def _():
+            for part in parts:
+                plane_copy(part, p, plane).start()
+
+        return 0
+
+    lax.fori_loop(0, planes, from_beside, 0)
+    for p in order[:-1]:
+        for part in parts:
+            plane_copy(part, p, p).wait_recv()
+    finish(
+        [[part[4].at[plane] for part in parts]]
+        + [[part[5].at[p] for part in parts] for p in order[:-1]]
+    )
+    for p in order:
+        for part in parts:
+            core_copy(part, p).wait_send()
+            beside_copy(part, p).wait_send()
+    for p in order[:-1]:
+        for part in parts:
+            plane_copy(part, p, plane).wait_send()
+
+
+def reduce_scratch(planes, rows, width, dtype):
+    return [
+        pltpu.VMEM((planes, ROW, rows, width), dtype),
+        pltpu.VMEM((planes, ROW, rows, width), dtype),
+        pltpu.VMEM((planes, rows, width), dtype),
+        pltpu.VMEM((planes, rows, width), dtype),
+        pltpu.VMEM((planes, rows, width), dtype),
+        pltpu.SemaphoreType.DMA((6, planes)),
+    ]
+
+
+STATS = 128
+
+
+def weigh(stats):
+    half = STATS // 2
+    tops = [stat[:, :half] for stat in stats]
+    top = functools.reduce(jnp.maximum, tops)
+    factors = [jnp.exp2(one - top) for one in tops]
+    total = sum(stat[:, half:] * factor for stat, factor in zip(stats, factors))
+    return top, factors, total
+
+
+def combine_kernel(n, numer_ref, stat_ref, cols_ref, *scratch):
+    numer_scratch, stat_scratch = scratch[:6], scratch[6:12]
+    piece_ref, swap_send, swap_recv, own_sem = scratch[12:]
+    me, plane, x, core = place(n)
+    planes = n // (CORES * ROW)
+    width = numer_ref.shape[-1]
+    heads = width // HEAD_SIZE
+    others = [lax.rem(me + step, n) for step in range(1, n)]
+    greet(others)
+
+    def merge(one, two, out):
+        top, factors, total = weigh([one[1][...], two[1][...]])
+        out[1][...] = jnp.concatenate([top, total], axis=1)
+        for head in range(heads):
+            at = slice(head * HEAD_SIZE, (head + 1) * HEAD_SIZE)
+            out[0][:, at] = (
+                one[0][:, at].astype(jnp.float32) * factors[0][:, head : head + 1]
+                + two[0][:, at].astype(jnp.float32) * factors[1][:, head : head + 1]
+            ).astype(out[0].dtype)
+
+    def finish(sources):
+        _, factors, total = weigh([source[1][...] for source in sources])
+        out = []
+        for head in range(heads):
+            at = slice(head * HEAD_SIZE, (head + 1) * HEAD_SIZE)
+            numer = sum(
+                source[0][:, at].astype(jnp.float32) * factor[:, head : head + 1]
+                for source, factor in zip(sources, factors)
+            )
+            out.append((numer / total[:, head : head + 1]).astype(jnp.bfloat16))
+        attn = jnp.concatenate(out, axis=1)
+        share = width // n
+        for device in range(n):
+            piece_ref[device] = attn[:, device * share : (device + 1) * share]
+
+    reduce_rows(
+        (plane, x, core, planes),
+        [(numer_ref, *numer_scratch), (stat_ref, *stat_scratch)],
+        merge,
+        finish,
+    )
+
+    def swap(device, slot):
+        return remote(
+            piece_ref.at[device], cols_ref.at[slot], swap_send.at[device], swap_recv.at[slot], device
+        )
+
+    own = pltpu.make_async_copy(piece_ref.at[me], cols_ref.at[me], own_sem)
+    own.start()
+    for device in others:
+        swap(device, me).start()
+    own.wait()
+    for device in others:
+        swap(device, device).wait_recv()
+    for device in others:
+        swap(device, me).wait_send()
+
+
+def combine(numer, stats, n):
+    qtok, width = numer.shape
+    planes, rows = n // (CORES * ROW), qtok // n
+    cols = pl.pallas_call(
+        functools.partial(combine_kernel, n),
+        out_shape=jax.ShapeDtypeStruct((n, rows, width // n), jnp.bfloat16),
+        in_specs=[pl.BlockSpec(memory_space=pltpu.VMEM)] * 2,
+        out_specs=pl.BlockSpec(memory_space=pltpu.VMEM),
+        scratch_shapes=reduce_scratch(planes, rows, width, jnp.bfloat16)
+        + reduce_scratch(planes, rows, STATS, jnp.float32)
+        + [
+            pltpu.VMEM((n, rows, width // n), jnp.bfloat16),
+            pltpu.SemaphoreType.DMA((n,)),
+            pltpu.SemaphoreType.DMA((n,)),
+            pltpu.SemaphoreType.DMA,
+        ],
+        compiler_params=pltpu.CompilerParams(
+            collective_id=1, has_side_effects=True, vmem_limit_bytes=40 * 2**20
+        ),
+        name="combine",
+    )(
+        numer.reshape(planes, ROW, CORES, rows, width),
+        stats.reshape(planes, ROW, CORES, rows, STATS),
+    )
+    return cols.reshape(qtok, width // n)
+
+
+TILE = 512
+
+
+def project_kernel(n, cols_ref, weight_ref, out_ref, part_ref, *scratch):
+    _, plane, x, core = place(n)
+    planes = n // (CORES * ROW)
+    rows, width = out_ref.shape
+    greet(
+        [index_of(lax.rem(plane + step, planes), x, core) for step in range(1, planes)]
+        + [index_of(plane, 1 - x, core), index_of(plane, x, 1 - core)]
+    )
+
+    def tile_step(tile, _):
+        at = pl.ds(pl.multiple_of(tile * TILE, TILE), TILE)
+        product = jnp.dot(cols_ref[...], weight_ref[:, at], preferred_element_type=jnp.float32)
+        part_ref[:, :, :, :, at] = product.astype(part_ref.dtype).reshape(
+            planes, ROW, CORES, rows, TILE
+        )
+        return 0
+
+    lax.fori_loop(0, width // TILE, tile_step, 0)
+
+    def merge(one, two, out):
+        out[0][...] = (one[0][...].astype(jnp.float32) + two[0][...].astype(jnp.float32)).astype(
+            out[0].dtype
+        )
+
+    def finish(sources):
+        out_ref[...] = sum(source[0][...].astype(jnp.float32) for source in sources).astype(
+            out_ref.dtype
+        )
+
+    reduce_rows((plane, x, core, planes), [(part_ref, *scratch)], merge, finish)
+
+
+def project(cols, weight, n):
+    qtok = cols.shape[0]
+    width = weight.shape[1]
+    planes, rows = n // (CORES * ROW), qtok // n
+    return pl.pallas_call(
+        functools.partial(project_kernel, n),
+        out_shape=jax.ShapeDtypeStruct((rows, width), jnp.bfloat16),
+        in_specs=[pl.BlockSpec(memory_space=pltpu.VMEM)] * 2,
+        out_specs=pl.BlockSpec(memory_space=pltpu.VMEM),
+        scratch_shapes=[pltpu.VMEM((planes, ROW, CORES, rows, width), jnp.bfloat16)]
+        + reduce_scratch(planes, rows, width, jnp.bfloat16),
+        compiler_params=pltpu.CompilerParams(
+            collective_id=2, has_side_effects=True, vmem_limit_bytes=40 * 2**20
+        ),
+        name="project",
+    )(cols, weight)
+
+
+def shards_near(n, queries, keys, values, block_mask, out_weight):
+    whole = gather_rows(queries, n)
+    qtok = whole.shape[0]
+    numer, top, total = attend(whole, keys, values, block_mask, jnp.bfloat16)
+    top, total = by_token(top, qtok), by_token(total, qtok)
+    room = ((0, 0), (0, STATS // 2 - top.shape[1]))
+    stats = jnp.concatenate([jnp.pad(top, room), jnp.pad(total, room)], axis=1)
+    cols = combine(numer, stats, n)
+    return project(cols, out_weight, n)
+
+
 def solution(mesh):
+    n = mesh.shape["ctx"]
+
+    def shards(queries, *rest):
+        fits = n % (CORES * ROW) == 0 and queries.shape[0] % 16 == 0
+        if fits and queries.shape[1] // HEAD_SIZE <= STATS // 2:
+            return shards_near(n, queries, *rest)
+        return shards_any(queries, *rest)
+
     return jax.shard_map(
-        shards_any,
+        shards,
         mesh=mesh,
         in_specs=(
             P(("groups", "ctx"), None),

time: 400 us -> 143 us (0.36)
  waiting for transfers between devices: 252 us -> 0 us
  Pallas kernels: 31.4 us -> 133 us
  blocking collectives: 77.4 us -> 0 us
  between operations: 13.2 us -> 0.12 us
  other arithmetic: 7.18 us -> 0.01 us
  local copies, waits for them, and re-layouts: 15.3 us -> 10.5 us
    reduce_scatter x3 -> x0, waiting for transfers between devices: 203 us -> none  [the longest x1 81.4 us: shards_any(): num_rows = lax.psum_scatter(numer, 'ctx', scatter_dimension=0, tiled=True)]
    pallas_call x0 -> x3, Pallas kernels: none -> 114 us  [the longest x1 55 us: combine(): pl.pallas_call(functools.partial(combine_kernel, n), out_shape=jax.ShapeD...]
    pmax x1 -> x0, blocking collectives: 65 us -> none  [shards_any(): rescale = by_token(jnp.exp2(top - lax.pmax(top, 'ctx')), qtok)]
    all_gather x1 -> x0, waiting for transfers between devices: 48.3 us -> none  [shards_any(): whole = lax.all_gather(queries, 'ctx', axis=0, tiled=True)]
    all_to_all x1 -> x0, blocking collectives: 12.4 us -> none  [shards_any(): lax.all_to_all(attn_rows.astype(jnp.bfloat16), 'ctx', split_axis=1, conca...]
    pallas_call x1, Pallas kernels: 31.4 us -> 19.5 us  [attend(): pl.pallas_call(attend_kernel, grid=(heads_kv,), out_shape=(jax.ShapeDtype...]
    unnamed x16 -> x15, local copies, waits for them, and re-layouts: 10.3 us -> 10.3 us
  transfers between devices with their start and end apart: 4 -> 0, of which waited for: 4 -> 0; matrix products, arithmetic and copies ran while one was open for 1% -> 0% of each run, Pallas kernels for 0% -> 0%
where the time goes in v2:
time: 143 us; the launch traced here: 144 us
  Pallas kernels  133 us (93%)
  local copies, waits for them, and re-layouts  10.5 us (7%)
    pallas_call x1, Pallas kernels, combine(): pl.pallas_call(functools.partial(combine_kernel, n), out_shape=jax.ShapeD...  55 us
    pallas_call x1, Pallas kernels, gather_rows(): pl.pallas_call(functools.partial(gather_kernel, n), out_shape=jax.ShapeDt...  29.5 us
    pallas_call x1, Pallas kernels, project(): pl.pallas_call(functools.partial(project_kernel, n), out_shape=jax.ShapeD...  29.3 us
    pallas_call x1, Pallas kernels, attend(): pl.pallas_call(attend_kernel, grid=(heads_kv,), out_shape=(jax.ShapeDtype...  19.5 us
    unnamed x15, local copies, waits for them, and re-layouts  10.3 us

profile of v2, /device:TPU:0, one launch (start us, length us, event | category | flops | bytes accessed | tf_op | source)
XLA Modules:
  0.0 143.9 jit_solution(7829941909766374613)
XLA Ops:
  0.0 29.5 %gather_rows.1 = bf16[16,16,5120]{2,1,0:T(8,128)(2,1)} custom-call(bf16[16,5120]{1,0:T(8,128)(2,1)} %own_ref.1), custom_call_target="tpu_custom_call" | custom-call | tf_op jit(solution)/shard_map/gather_rows/pallas_call | solution.py:226
  29.5 0.0 copy-start
  29.5 1.7 %copy-done = bf16[16,16,5120]{2,1,0:T(8,128)(2,1)S(1)} copy-done((bf16[16,16,5120]{2,1,0:T(8,128)(2,1)S(1)}, bf16[16,16,5120]{2,1,0:T(8,128)(2,1)}, u32[]{:S(2)}) %copy-start) | copy-done | bytes 2621464
  31.2 0.0 copy-start.2
  31.2 1.9 %copy-done.2 = bf16[1536,1024]{1,0:T(8,128)(2,1)S(1)} copy-done((bf16[1536,1024]{1,0:T(8,128)(2,1)S(1)}, bf16[1536,1024]{1,0:T(8,128)(2,1)}, u32[]{:S(2)}) %copy-start.2) | copy-done | bytes 3145752
  33.1 0.0 copy-start.3
  33.1 1.9 %copy-done.3 = bf16[1536,1024]{1,0:T(8,128)(2,1)S(1)} copy-done((bf16[1536,1024]{1,0:T(8,128)(2,1)S(1)}, bf16[1536,1024]{1,0:T(8,128)(2,1)}, u32[]{:S(2)}) %copy-start.3) | copy-done | bytes 3145752
  35.0 0.0 copy-start.6
  35.0 0.7 copy-done.6
  35.7 19.5 %attend.1 = (bf16[256,5120]{1,0:T(8,128)(2,1)S(1)}, f32[8,2,640]{2,1,0:T(2,128)S(1)}, f32[8,2,640]{2,1,0:T(2,128)S(1)}) custom-call(s32[8,2,12]{2,1,0:T(2,128)S(1)} %copy-done.6, bf16[256,5120]{1,0:T(8,128)(2,1)S(1)} %bitcast.22, bf16[1536,1024]{1,0:T(8,128)(2,1)S(1)} %copy-done.2, bf16[1536,1024]{1,0:T(8,128)(2,1)S(1)} %copy-done.3), custom_call_target="tpu_custom_call" | custom-call | tf_op jit(solution)/shard_map/attend/pallas_call | solution.py:92
  55.3 0.0 copy-start.4
  55.3 1.5 %copy-done.4 = bf16[256,5120]{1,0:T(8,128)(2,1)} copy-done((bf16[256,5120]{1,0:T(8,128)(2,1)}, bf16[256,5120]{1,0:T(8,128)(2,1)S(1)}, u32[]{:S(2)}) %copy-start.4) | copy-done | bytes 2621464
  56.8 0.0 copy-start.1
  56.9 0.1 copy.12
  57.0 0.0 copy-start.5
  57.0 1.9 %copy-done.5 = bf16[256,5120]{1,0:T(8,128)(2,1)S(1)} copy-done((bf16[256,5120]{1,0:T(8,128)(2,1)S(1)}, bf16[256,5120]{1,0:T(8,128)(2,1)}, u32[]{:S(2)}) %copy-start.5) | copy-done | bytes 2621464
  58.9 55.0 %combine.1 = bf16[16,16,320]{2,1,0:T(8,128)(2,1)S(1)} custom-call(bf16[4,2,2,16,5120]{4,3,2,1,0:T(8,128)(2,1)S(1)} %bitcast.23, f32[4,2,2,16,128]{4,3,2,1,0:T(8,128)S(1)} %bitcast.25), custom_call_target="tpu_custom_call" | custom-call | tf_op jit(solution)/shard_map/combine/pallas_call | solution.py:404
  113.9 0.0 copy-done.1
  113.9 29.3 %project.1 = bf16[16,5120]{1,0:T(8,128)(2,1)S(1)} custom-call(bf16[256,320]{1,0:T(8,128)(2,1)S(1)} %bitcast.24, bf16[320,5120]{1,0:T(8,128)(2,1)S(1)} %copy-done.1), custom_call_target="tpu_custom_call" | custom-call | tf_op jit(solution)/shard_map/project/pallas_call | solution.py:467
  143.2 0.7 copy.18
  (8 shorter events, 0.1 us)
Async XLA Ops:
  29.5 1.7 %copy-start = (bf16[16,16,5120]{2,1,0:T(8,128)(2,1)S(1)}, bf16[16,16,5120]{2,1,0:T(8,128)(2,1)}, u32[]{:S(2)}) copy-start(bf16[16,16,5120]{2,1,0:T(8,128)(2,1)} %gather_rows.1) | copy-start | bytes 7864324
  31.2 1.9 %copy-start.2 = (bf16[1536,1024]{1,0:T(8,128)(2,1)S(1)}, bf16[1536,1024]{1,0:T(8,128)(2,1)}, u32[]{:S(2)}) copy-start(bf16[1536,1024]{1,0:T(8,128)(2,1)} %k_ref.1) | copy-start | bytes 9437188
  33.1 1.9 %copy-start.3 = (bf16[1536,1024]{1,0:T(8,128)(2,1)S(1)}, bf16[1536,1024]{1,0:T(8,128)(2,1)}, u32[]{:S(2)}) copy-start(bf16[1536,1024]{1,0:T(8,128)(2,1)} %v_ref.1) | copy-start | bytes 9437188
  35.0 0.7 copy-start.6
  55.3 1.5 %copy-start.4 = (bf16[256,5120]{1,0:T(8,128)(2,1)}, bf16[256,5120]{1,0:T(8,128)(2,1)S(1)}, u32[]{:S(2)}) copy-start(bf16[256,5120]{1,0:T(8,128)(2,1)S(1)} %get-tuple-element.8) | copy-start | bytes 7864324
  56.8 57.1 %copy-start.1 = (bf16[320,5120]{1,0:T(8,128)(2,1)S(1)}, bf16[320,5120]{1,0:T(8,128)(2,1)}, u32[]{:S(2)}) copy-start(bf16[320,5120]{1,0:T(8,128)(2,1)} %weight_ref.1) | copy-start | bytes 9830404
  57.0 1.9 %copy-start.5 = (bf16[256,5120]{1,0:T(8,128)(2,1)S(1)}, bf16[256,5120]{1,0:T(8,128)(2,1)}, u32[]{:S(2)}) copy-start(bf16[256,5120]{1,0:T(8,128)(2,1)} %copy-done.4) | copy-start | bytes 7864324

commit v3 on v2

--- a/solution.py
+++ b/solution.py
@@ -12,9 +12,11 @@
 NEG = -1e30
 LOG2E = math.log2(math.e)
 MESH = pl.DeviceIdType.MESH
-
-
-def attend_kernel(mask_ref, q_ref, k_ref, v_ref, numer_ref, top_ref, total_ref, live_ref, score_ref):
+CORES, ROW = 2, 2
+
+
+def attend_kernel(rows_each, mask_ref, q_ref, k_ref, v_ref, *refs):
+    *numer_refs, top_ref, total_ref, live_ref, score_ref = refs
     head = pl.program_id(0)
     query_blocks, key_blocks = mask_ref.shape[1:]
     key_block = k_ref.shape[0] // key_blocks
@@ -76,12 +78,21 @@
         total_ref[0, at : at + 1, :] = jnp.sum(total, axis=0, keepdims=True)
         for g in range(group):
             columns = slice(g * query_block, (g + 1) * query_block)
-            numer_ref[rows, g * HEAD_SIZE : (g + 1) * HEAD_SIZE] = numer[:, columns].T.astype(
-                numer_ref.dtype
-            )
-
-
-def attend(whole, keys, values, block_mask, numer_type):
+            out_columns = slice(g * HEAD_SIZE, (g + 1) * HEAD_SIZE)
+            tokens = numer[:, columns].T
+            if not rows_each:
+                numer_refs[0][rows, out_columns] = tokens
+                continue
+            tokens = tokens.reshape(-1, CORES, rows_each, HEAD_SIZE)
+            first = lax.rem(lax.axis_index("ctx"), CORES) == 0
+            half = pl.ds(at * query_block // CORES, query_block // CORES)
+            kept = jnp.where(first, tokens[:, 0], tokens[:, 1]).reshape(-1, HEAD_SIZE)
+            sent = jnp.where(first, tokens[:, 1], tokens[:, 0]).reshape(-1, HEAD_SIZE)
+            numer_refs[0][half, out_columns] = kept
+            numer_refs[1][half, out_columns] = sent.astype(jnp.bfloat16)
+
+
+def attend(whole, keys, values, block_mask, rows_each):
     qtok, width = whole.shape
     kdev = keys.shape[0]
     heads_kv, query_blocks, key_blocks = block_mask.shape
@@ -89,22 +100,29 @@
     lanes = columns // HEAD_SIZE * (qtok // query_blocks)
     stat = jax.ShapeDtypeStruct((heads_kv, query_blocks, lanes), jnp.float32)
     stat_spec = pl.BlockSpec((1, query_blocks, lanes), lambda h: (h, 0, 0))
+    numers = [jax.ShapeDtypeStruct((qtok, width), jnp.float32)]
+    if rows_each:
+        numers = [jax.ShapeDtypeStruct((qtok // CORES, width), t) for t in (jnp.float32, jnp.bfloat16)]
     return pl.pallas_call(
-        attend_kernel,
+        functools.partial(attend_kernel, rows_each),
         grid=(heads_kv,),
-        out_shape=(jax.ShapeDtypeStruct((qtok, width), numer_type), stat, stat),
+        out_shape=(*numers, stat, stat),
         in_specs=[
             pl.BlockSpec(memory_space=pltpu.SMEM),
             pl.BlockSpec((qtok, columns), lambda h: (0, h)),
             pl.BlockSpec((kdev, HEAD_SIZE), lambda h: (0, h)),
             pl.BlockSpec((kdev, HEAD_SIZE), lambda h: (0, h)),
         ],
-        out_specs=(pl.BlockSpec((qtok, columns), lambda h: (0, h)), stat_spec, stat_spec),
+        out_specs=(
+            *(pl.BlockSpec((numer.shape[0], columns), lambda h: (0, h)) for numer in numers),
+            stat_spec,
+            stat_spec,
+        ),
         scratch_shapes=[
             pltpu.SMEM((key_blocks + 2,), jnp.int32),
             pltpu.VMEM(((key_blocks + 1) // 2, 2 * kdev // key_blocks, lanes), jnp.float32),
         ],
-        compiler_params=pltpu.CompilerParams(vmem_limit_bytes=40 * 2**20),
+        compiler_params=pltpu.CompilerParams(vmem_limit_bytes=60 * 2**20),
         name="attend",
     )(block_mask, whole, keys, values)
 
@@ -118,7 +136,7 @@
 def shards_any(queries, keys, values, block_mask, out_weight):
     whole = lax.all_gather(queries, "ctx", axis=0, tiled=True)
     qtok, width = whole.shape
-    numer, top, total = attend(whole, keys, values, block_mask, jnp.float32)
+    numer, top, total = attend(whole, keys, values, block_mask, 0)
     rescale = by_token(jnp.exp2(top - lax.pmax(top, "ctx")), qtok)
     denom = by_token(total, qtok) * rescale
     numer = (numer.reshape(qtok, -1, HEAD_SIZE) * rescale[:, :, None]).reshape(qtok, width)
@@ -140,9 +158,6 @@
     return summed.astype(jnp.bfloat16)
 
 
-CORES, ROW = 2, 2
-
-
 def place(n):
     me = lax.axis_index("ctx")
     core = lax.rem(me, CORES)
@@ -177,47 +192,95 @@
     me, plane, x, core = place(n)
     planes = n // (CORES * ROW)
     beside, sibling = 1 - x, 1 - core
-    across = [lax.rem(plane + step, planes) for step in range(1, planes)]
-    greet(
-        [index_of(p, x, core) for p in across]
-        + [index_of(plane, beside, core), index_of(plane, x, sibling)]
-    )
+    barrier = pltpu.get_barrier_semaphore()
+
+    def hello(device):
+        pl.semaphore_signal(barrier, inc=1, device_id={"ctx": device}, device_id_type=MESH)
+
+    hello(index_of(plane, beside, core))
+    hello(index_of(plane, x, sibling))
+
+    @pl.when(plane > 0)
+    def _():
+        hello(index_of(plane - 1, x, core))
+
+    @pl.when(plane < planes - 1)
+    def _():
+        hello(index_of(plane + 1, x, core))
+
+    ends = (plane > 0).astype(jnp.int32) + (plane < planes - 1).astype(jnp.int32)
+    pl.semaphore_wait(barrier, 2 + ends)
     own = pltpu.make_async_copy(own_ref, whole_ref.at[me], own_sem)
     own.start()
-    sends = []
-
-    def send(src, block, slot, device):
-        copy = remote(src, whole_ref.at[block], send_sem.at[slot], recv_sem.at[block], device)
-        copy.start()
-        sends.append(copy)
-
-    def arrived(block, device):
-        remote(own_ref, whole_ref.at[block], send_sem.at[0], recv_sem.at[block], device).wait_recv()
-
-    slot = 0
-    for p in across:
-        send(own_ref, me, slot, index_of(p, x, core))
-        slot += 1
-    send(own_ref, me, slot, index_of(plane, beside, core))
-    send(own_ref, me, slot + 1, index_of(plane, x, sibling))
-    slot += 2
-    for step in range(planes):
-        if step:
-            block = index_of(lax.rem(plane + planes - step, planes), x, core)
-            arrived(block, me)
-            send(whole_ref.at[block], block, slot, index_of(plane, beside, core))
-            send(whole_ref.at[block], block, slot + 1, index_of(plane, x, sibling))
-            slot += 2
-    for step in range(planes):
-        block = index_of(lax.rem(plane + planes - step, planes), beside, core)
-        arrived(block, me)
-        send(whole_ref.at[block], block, slot, index_of(plane, x, sibling))
-        slot += 1
-    for step in range(planes):
-        for side in (x, beside):
-            arrived(index_of(lax.rem(plane + planes - step, planes), side, sibling), me)
-    for copy in sends:
-        copy.wait_send()
+
+    def copy_to(block, way, device, mine=False):
+        src = own_ref if mine else whole_ref.at[block]
+        return remote(src, whole_ref.at[block], send_sem.at[way, block], recv_sem.at[block], device)
+
+    def arrived(block):
+        copy_to(block, 0, me).wait_recv()
+
+    def pass_on(p, up, act, mine=False):
+        block = index_of(p, x, core)
+
+        @pl.when(plane + up < planes if up > 0 else plane + up >= 0)
+        def _():
+            act(copy_to(block, 0 if up > 0 else 1, index_of(plane + up, x, core), mine))
+
+    start, ended = (lambda copy: copy.start()), (lambda copy: copy.wait_send())
+    pass_on(plane, 1, start, True)
+    pass_on(plane, -1, start, True)
+    copy_to(me, 2, index_of(plane, beside, core), True).start()
+    copy_to(me, 3, index_of(plane, x, sibling), True).start()
+    for distance in range(1, planes):
+        for up in (1, -1):
+            p = plane - up * distance
+
+            @pl.when(p >= 0 if up > 0 else p < planes)
+            def _():
+                block = index_of(p, x, core)
+                arrived(block)
+                pass_on(p, up, start)
+                copy_to(block, 2, index_of(plane, beside, core)).start()
+                copy_to(block, 3, index_of(plane, x, sibling)).start()
+
+    def near_first(act):
+        act(plane)
+        for distance in range(1, planes):
+            for up in (1, -1):
+                p = plane - up * distance
+
+                @pl.when(p >= 0 if up > 0 else p < planes)
+                def _():
+                    act(p)
+
+    def from_beside(p):
+        block = index_of(p, beside, core)
+        arrived(block)
+        copy_to(block, 3, index_of(plane, x, sibling)).start()
+
+    def from_sibling(p):
+        arrived(index_of(p, x, sibling))
+        arrived(index_of(p, beside, sibling))
+
+    near_first(from_beside)
+    near_first(from_sibling)
+    pass_on(plane, 1, ended, True)
+    pass_on(plane, -1, ended, True)
+    for distance in range(1, planes):
+        for up in (1, -1):
+            p = plane - up * distance
+
+            @pl.when(p >= 0 if up > 0 else p < planes)
+            def _():
+                pass_on(p, up, ended)
+
+    def sent(p):
+        copy_to(index_of(p, x, core), 2, index_of(plane, beside, core)).wait_send()
+        copy_to(index_of(p, x, core), 3, index_of(plane, x, sibling)).wait_send()
+        copy_to(index_of(p, beside, core), 3, index_of(plane, x, sibling)).wait_send()
+
+    near_first(sent)
     own.wait()
 
 
@@ -230,7 +293,7 @@
         out_specs=pl.BlockSpec(memory_space=pltpu.VMEM),
         scratch_shapes=[
             pltpu.SemaphoreType.DMA,
-            pltpu.SemaphoreType.DMA((n,)),
+            pltpu.SemaphoreType.DMA((4, n)),
             pltpu.SemaphoreType.DMA((n,)),
         ],
         compiler_params=pltpu.CompilerParams(collective_id=0, has_side_effects=True),
@@ -242,77 +305,73 @@
 def reduce_rows(place_of, parts, merge, finish):
     plane, x, core, planes = place_of
     beside, sibling = 1 - x, 1 - core
-    order = [lax.rem(plane + step, planes) for step in range(1, planes)] + [plane]
-
-    def core_copy(part, p):
-        src, got, _, _, _, _, sem = part
-        return remote(
-            src.at[p, :, sibling], got.at[p], sem.at[0, p], sem.at[1, p], index_of(plane, x, sibling)
-        )
-
-    def beside_copy(part, p):
-        _, _, held, got, _, _, sem = part
-        return remote(
-            held.at[p, beside], got.at[p], sem.at[2, p], sem.at[3, p], index_of(plane, beside, core)
-        )
-
-    def plane_copy(part, p, slot):
-        _, _, _, _, summed, got, sem = part
-        return remote(summed.at[p], got.at[slot], sem.at[4, p], sem.at[5, slot], index_of(p, x, core))
-
-    for p in order:
-        for part in parts:
-            core_copy(part, p).start()
+    others = [lax.rem(plane + step, planes) for step in range(1, planes)]
 
     def turn(step):
         return lax.rem(plane + 1 + step, planes)
 
+    def core_copy(part, p):
+        sem = part[9]
+        return remote(
+            part[0](p), part[2].at[p], sem.at[0, p], sem.at[1, p], index_of(plane, x, sibling)
+        )
+
+    def beside_copy(part, p):
+        sem = part[9]
+        return remote(
+            part[3].at[p], part[5].at[p], sem.at[2, p], sem.at[3, p], index_of(plane, beside, core)
+        )
+
+    def plane_copy(part, p, slot):
+        sem = part[9]
+        return remote(
+            part[6].at[p], part[8].at[slot], sem.at[4, p], sem.at[5, slot], index_of(p, x, core)
+        )
+
+    for p in others + [plane]:
+        for part in parts:
+            core_copy(part, p).start()
+
     def from_core(step, _):
         p = turn(step)
         for part in parts:
             core_copy(part, p).wait_recv()
-        for side in range(ROW):
+        for side, out in ((beside, 3), (x, 4)):
             merge(
-                [part[0].at[p, side, core] for part in parts],
-                [part[1].at[p, side] for part in parts],
+                [part[1](p, side) for part in parts],
                 [part[2].at[p, side] for part in parts],
+                [part[out].at[p] for part in parts],
             )
-        for part in parts:
-            beside_copy(part, p).start()
+            if out == 3:
+                for part in parts:
+                    beside_copy(part, p).start()
         return 0
 
     lax.fori_loop(0, planes, from_core, 0)
 
-    def from_beside(step, _):
+    def from_beside(p, outs):
+        for part in parts:
+            beside_copy(part, p).wait_recv()
+        merge([part[4].at[p] for part in parts], [part[5].at[p] for part in parts], outs)
+
+    def to_plane(step, _):
         p = turn(step)
-        for part in parts:
-            beside_copy(part, p).wait_recv()
-        merge(
-            [part[2].at[p, x] for part in parts],
-            [part[3].at[p] for part in parts],
-            [part[4].at[p] for part in parts],
-        )
-
-        @pl.when(step < planes - 1)
-        def _():
-            for part in parts:
-                plane_copy(part, p, plane).start()
-
+        from_beside(p, [part[6].at[p] for part in parts])
+        for part in parts:
+            plane_copy(part, p, plane).start()
         return 0
 
-    lax.fori_loop(0, planes, from_beside, 0)
-    for p in order[:-1]:
+    lax.fori_loop(0, planes - 1, to_plane, 0)
+    from_beside(plane, [part[7] for part in parts])
+    for p in others:
         for part in parts:
             plane_copy(part, p, p).wait_recv()
-    finish(
-        [[part[4].at[plane] for part in parts]]
-        + [[part[5].at[p] for part in parts] for p in order[:-1]]
-    )
-    for p in order:
+    finish([[part[7] for part in parts]] + [[part[8].at[p] for part in parts] for p in others])
+    for p in others + [plane]:
         for part in parts:
             core_copy(part, p).wait_send()
             beside_copy(part, p).wait_send()
-    for p in order[:-1]:
+    for p in others:
         for part in parts:
             plane_copy(part, p, plane).wait_send()
 
@@ -320,9 +379,11 @@
 def reduce_scratch(planes, rows, width, dtype):
     return [
         pltpu.VMEM((planes, ROW, rows, width), dtype),
-        pltpu.VMEM((planes, ROW, rows, width), dtype),
+        pltpu.VMEM((planes, rows, width), dtype),
+        pltpu.VMEM((planes, rows, width), jnp.float32),
         pltpu.VMEM((planes, rows, width), dtype),
         pltpu.VMEM((planes, rows, width), dtype),
+        pltpu.VMEM((rows, width), jnp.float32),
         pltpu.VMEM((planes, rows, width), dtype),
         pltpu.SemaphoreType.DMA((6, planes)),
     ]
@@ -340,12 +401,12 @@
     return top, factors, total
 
 
-def combine_kernel(n, numer_ref, stat_ref, cols_ref, *scratch):
-    numer_scratch, stat_scratch = scratch[:6], scratch[6:12]
-    piece_ref, swap_send, swap_recv, own_sem = scratch[12:]
+def combine_kernel(n, kept_ref, sent_ref, stat_ref, cols_ref, *scratch):
+    numer_scratch, stat_scratch = scratch[:8], scratch[8:16]
+    piece_ref, swap_send, swap_recv, own_sem = scratch[16:]
     me, plane, x, core = place(n)
     planes = n // (CORES * ROW)
-    width = numer_ref.shape[-1]
+    width = kept_ref.shape[-1]
     heads = width // HEAD_SIZE
     others = [lax.rem(me + step, n) for step in range(1, n)]
     greet(others)
@@ -377,7 +438,14 @@
 
     reduce_rows(
         (plane, x, core, planes),
-        [(numer_ref, *numer_scratch), (stat_ref, *stat_scratch)],
+        [
+            (lambda p: sent_ref.at[p], lambda p, side: kept_ref.at[p, side], *numer_scratch),
+            (
+                lambda p: stat_ref.at[p, :, 1 - core],
+                lambda p, side: stat_ref.at[p, side, core],
+                *stat_scratch,
+            ),
+        ],
         merge,
         finish,
     )
@@ -398,13 +466,13 @@
         swap(device, me).wait_send()
 
 
-def combine(numer, stats, n):
-    qtok, width = numer.shape
+def combine(kept, sent, stats, n):
+    qtok, width = stats.shape[0], kept.shape[1]
     planes, rows = n // (CORES * ROW), qtok // n
     cols = pl.pallas_call(
         functools.partial(combine_kernel, n),
         out_shape=jax.ShapeDtypeStruct((n, rows, width // n), jnp.bfloat16),
-        in_specs=[pl.BlockSpec(memory_space=pltpu.VMEM)] * 2,
+        in_specs=[pl.BlockSpec(memory_space=pltpu.VMEM)] * 3,
         out_specs=pl.BlockSpec(memory_space=pltpu.VMEM),
         scratch_shapes=reduce_scratch(planes, rows, width, jnp.bfloat16)
         + reduce_scratch(planes, rows, STATS, jnp.float32)
@@ -419,7 +487,8 @@
         ),
         name="combine",
     )(
-        numer.reshape(planes, ROW, CORES, rows, width),
+        kept.reshape(planes, ROW, rows, width),
+        sent.reshape(planes, ROW, rows, width),
         stats.reshape(planes, ROW, CORES, rows, STATS),
     )
     return cols.reshape(qtok, width // n)
@@ -428,7 +497,7 @@
 TILE = 512
 
 
-def project_kernel(n, cols_ref, weight_ref, out_ref, part_ref, *scratch):
+def project_kernel(n, cols_ref, weight_ref, out_ref, kept_ref, sent_ref, *scratch):
     _, plane, x, core = place(n)
     planes = n // (CORES * ROW)
     rows, width = out_ref.shape
@@ -440,9 +509,10 @@
     def tile_step(tile, _):
         at = pl.ds(pl.multiple_of(tile * TILE, TILE), TILE)
         product = jnp.dot(cols_ref[...], weight_ref[:, at], preferred_element_type=jnp.float32)
-        part_ref[:, :, :, :, at] = product.astype(part_ref.dtype).reshape(
-            planes, ROW, CORES, rows, TILE
-        )
+        product = product.reshape(planes, ROW, CORES, rows, TILE)
+        kept_ref[:, :, :, at] = jnp.where(core == 0, product[:, :, 0], product[:, :, 1])
+        sent = jnp.where(core == 0, product[:, :, 1], product[:, :, 0])
+        sent_ref[:, :, :, at] = sent.astype(sent_ref.dtype)
         return 0
 
     lax.fori_loop(0, width // TILE, tile_step, 0)
@@ -457,7 +527,7 @@
             out_ref.dtype
         )
 
-    reduce_rows((plane, x, core, planes), [(part_ref, *scratch)], merge, finish)
+    reduce_rows((plane, x, core, planes), [(lambda p: sent_ref.at[p], lambda p, side: kept_ref.at[p, side], *scratch)], merge, finish)
 
 
 def project(cols, weight, n):
@@ -469,7 +539,7 @@
         out_shape=jax.ShapeDtypeStruct((rows, width), jnp.bfloat16),
         in_specs=[pl.BlockSpec(memory_space=pltpu.VMEM)] * 2,
         out_specs=pl.BlockSpec(memory_space=pltpu.VMEM),
-        scratch_shapes=[pltpu.VMEM((planes, ROW, CORES, rows, width), jnp.bfloat16)]
+        scratch_shapes=[pltpu.VMEM((planes, ROW, rows, width), t) for t in (jnp.float32, jnp.bfloat16)]
         + reduce_scratch(planes, rows, width, jnp.bfloat16),
         compiler_params=pltpu.CompilerParams(
             collective_id=2, has_side_effects=True, vmem_limit_bytes=40 * 2**20
@@ -481,11 +551,11 @@
 def shards_near(n, queries, keys, values, block_mask, out_weight):
     whole = gather_rows(queries, n)
     qtok = whole.shape[0]
-    numer, top, total = attend(whole, keys, values, block_mask, jnp.bfloat16)
+    kept, sent, top, total = attend(whole, keys, values, block_mask, queries.shape[0])
     top, total = by_token(top, qtok), by_token(total, qtok)
     room = ((0, 0), (0, STATS // 2 - top.shape[1]))
     stats = jnp.concatenate([jnp.pad(top, room), jnp.pad(total, room)], axis=1)
-    cols = combine(numer, stats, n)
+    cols = combine(kept, sent, stats, n)
     return project(cols, out_weight, n)
 
 
@@ -493,7 +563,7 @@
     n = mesh.shape["ctx"]
 
     def shards(queries, *rest):
-        fits = n % (CORES * ROW) == 0 and queries.shape[0] % 16 == 0
+        fits = n % (CORES * ROW) == 0 and queries.shape[0] == 16
         if fits and queries.shape[1] // HEAD_SIZE <= STATS // 2:
             return shards_near(n, queries, *rest)
         return shards_any(queries, *rest)

time: 143 us -> 131 us (0.916)
  Pallas kernels: 133 us -> 127 us
  local copies, waits for them, and re-layouts: 10.5 us -> 5.64 us
    pallas_call x1, Pallas kernels: 55 us -> 33.5 us  [combine(): pl.pallas_call(functools.partial(combine_kernel, n), out_shape=jax.ShapeD...]
    pallas_call x1, Pallas kernels: 19.5 us -> 37.1 us  [attend(): pl.pallas_call(functools.partial(attend_kernel, rows_each), grid=(heads_k...]
    unnamed x15 -> x7, local copies, waits for them, and re-layouts: 10.3 us -> 3.73 us
    pallas_call x1, Pallas kernels: 29.5 us -> 27.3 us  [gather_rows(): pl.pallas_call(functools.partial(gather_kernel, n), out_shape=jax.ShapeDt...]
    pallas_call x2, local copies, waits for them, and re-layouts: 0.01 us -> 1.73 us  [attend(): pl.pallas_call(functools.partial(attend_kernel, rows_each), grid=(heads_k...]
where the time goes in v3:
time: 131 us; the launch traced here: 133 us
  Pallas kernels  127 us (97%)
  local copies, waits for them, and re-layouts  5.64 us (4%)
    pallas_call x1, Pallas kernels, attend(): pl.pallas_call(functools.partial(attend_kernel, rows_each), grid=(heads_k...  37.1 us
    pallas_call x1, Pallas kernels, combine(): pl.pallas_call(functools.partial(combine_kernel, n), out_shape=jax.ShapeD...  33.5 us
    pallas_call x1, Pallas kernels, project(): pl.pallas_call(functools.partial(project_kernel, n), out_shape=jax.ShapeD...  29.5 us
    pallas_call x1, Pallas kernels, gather_rows(): pl.pallas_call(functools.partial(gather_kernel, n), out_shape=jax.ShapeDt...  27.3 us
    unnamed x7, local copies, waits for them, and re-layouts  3.73 us

profile of v3, /device:TPU:0, one launch (start us, length us, event | category | flops | bytes accessed | tf_op | source)
XLA Modules:
  0.0 133.2 jit_solution(10511766974220626495)
XLA Ops:
  0.0 27.3 %gather_rows.1 = bf16[16,16,5120]{2,1,0:T(8,128)(2,1)} custom-call(bf16[16,5120]{1,0:T(8,128)(2,1)} %own_ref.1), custom_call_target="tpu_custom_call" | custom-call | tf_op jit(solution)/shard_map/gather_rows/pallas_call | solution.py:289
  27.3 37.1 %attend.1 = (f32[128,5120]{1,0:T(8,128)}, bf16[128,5120]{1,0:T(8,128)(2,1)}, f32[8,2,640]{2,1,0:T(2,128)}, f32[8,2,640]{2,1,0:T(2,128)}) custom-call(s32[8,2,12]{2,1,0:T(2,128)} %mask_ref.1, bf16[256,5120]{1,0:T(8,128)(2,1)} %bitcast.27, bf16[1536,1024]{1,0:T(8,128)(2,1)} %k_ref.1, bf16[1536,1024]{1,0:T(8,128)(2,1)} %v_ref.1), custom_call_target="tpu_custom_call" | custom-call | tf_op jit(solution)/shard_map/attend/pallas_call | solution.py:106
  64.4 0.0 copy-start
  64.4 0.9 copy.8
  65.4 0.8 copy.10
  66.3 0.1 copy.12
  66.4 0.0 copy-start.1
  66.4 1.7 %copy-done.1 = f32[128,5120]{1,0:T(8,128)S(1)} copy-done((f32[128,5120]{1,0:T(8,128)S(1)}, f32[128,5120]{1,0:T(8,128)}, u32[]{:S(2)}) %copy-start.1) | copy-done | bytes 2621464
  68.1 0.0 copy-start.2
  68.1 1.3 copy-done.2
  69.4 33.5 %combine.1 = bf16[16,16,320]{2,1,0:T(8,128)(2,1)S(1)} custom-call(f32[4,2,16,5120]{3,2,1,0:T(8,128)S(1)} %bitcast.23, bf16[4,2,16,5120]{3,2,1,0:T(8,128)(2,1)S(1)} %bitcast.24, f32[4,2,2,16,128]{4,3,2,1,0:T(8,128)S(1)} %bitcast.26), custom_call_target="tpu_custom_call" | custom-call | tf_op jit(solution)/shard_map/combine/pallas_call | solution.py:472
  102.9 0.0 copy-done
  102.9 29.5 %project.1 = bf16[16,5120]{1,0:T(8,128)(2,1)S(1)} custom-call(bf16[256,320]{1,0:T(8,128)(2,1)S(1)} %bitcast.25, bf16[320,5120]{1,0:T(8,128)(2,1)S(1)} %copy-done), custom_call_target="tpu_custom_call" | custom-call | tf_op jit(solution)/shard_map/project/pallas_call | solution.py:537
  132.5 0.7 copy.18
  (6 shorter events, 0.1 us)
Async XLA Ops:
  64.4 38.5 %copy-start = (bf16[320,5120]{1,0:T(8,128)(2,1)S(1)}, bf16[320,5120]{1,0:T(8,128)(2,1)}, u32[]{:S(2)}) copy-start(bf16[320,5120]{1,0:T(8,128)(2,1)} %weight_ref.1) | copy-start | bytes 9830404
  66.4 1.7 %copy-start.1 = (f32[128,5120]{1,0:T(8,128)S(1)}, f32[128,5120]{1,0:T(8,128)}, u32[]{:S(2)}) copy-start(f32[128,5120]{1,0:T(8,128)} %get-tuple-element.9) | copy-start | bytes 7864324
  68.1 1.3 copy-start.2

commit v4 on v3

--- a/solution.py
+++ b/solution.py
@@ -10,19 +10,22 @@
 
 HEAD_SIZE = 128
 NEG = -1e30
+ONES = 16
 LOG2E = math.log2(math.e)
 MESH = pl.DeviceIdType.MESH
 CORES, ROW = 2, 2
 
 
 def attend_kernel(rows_each, mask_ref, q_ref, k_ref, v_ref, *refs):
-    *numer_refs, top_ref, total_ref, live_ref, score_ref = refs
+    *numer_refs, top_ref, total_ref, live_ref, score_ref, query_ref, value_ref, sum_ref = refs
     head = pl.program_id(0)
     query_blocks, key_blocks = mask_ref.shape[1:]
     key_block = k_ref.shape[0] // key_blocks
     query_block = q_ref.shape[0] // query_blocks
     group = q_ref.shape[1] // HEAD_SIZE
     factor = LOG2E / math.sqrt(HEAD_SIZE)
+    value_ref[:HEAD_SIZE] = v_ref[...].T
+    value_ref[HEAD_SIZE:] = jnp.ones((ONES, v_ref.shape[0]), jnp.bfloat16)
     for at in range(query_blocks):
         rows = pl.ds(at * query_block, query_block)
         count = jnp.int32(0)
@@ -30,52 +33,46 @@
             live_ref[count] = block
             count = count + (mask_ref[head, at, block] > 0).astype(jnp.int32)
         live_ref[count] = 0
-        stacked = jnp.concatenate(
-            [q_ref[rows, g * HEAD_SIZE : (g + 1) * HEAD_SIZE] for g in range(group)], axis=0
-        )
-        lanes = stacked.shape[0]
+        for g in range(group):
+            tokens = q_ref[rows, g * HEAD_SIZE : (g + 1) * HEAD_SIZE]
+            query_ref[:, g * query_block : (g + 1) * query_block] = tokens.T
+        lanes = query_ref.shape[1]
         pairs = (count + 1) // 2
 
-        def block_of(ref, which):
-            start = pl.multiple_of(live_ref[which] * key_block, key_block)
-            return ref[pl.ds(start, key_block), :]
+        def start_of(which):
+            return pl.multiple_of(live_ref[which] * key_block, key_block)
 
         def score_step(pair, top):
-            both = jnp.concatenate([block_of(k_ref, 2 * pair), block_of(k_ref, 2 * pair + 1)], axis=0)
-            scores = lax.dot_general(
-                both, stacked, (((1,), (1,)), ((), ())), preferred_element_type=jnp.float32
-            ) * factor
-            score_ref[pair] = scores
-            half = jnp.max(scores[:key_block].reshape(key_block // 8, 8, lanes), axis=0)
-            other = jnp.max(scores[key_block:].reshape(key_block // 8, 8, lanes), axis=0)
-            other = jnp.where(2 * pair + 1 < count, other, NEG)
-            return jnp.maximum(top, jnp.maximum(half, other))
+            tops = [top]
+            for half in range(2):
+                block = k_ref[pl.ds(start_of(2 * pair + half), key_block), :]
+                scores = jnp.dot(block, query_ref[...], preferred_element_type=jnp.float32)
+                score_ref[pair, half * key_block : (half + 1) * key_block] = scores
+                tops.append(jnp.max(scores.reshape(key_block // 8, 8, lanes), axis=0))
+            tops[2] = jnp.where(2 * pair + 1 < count, tops[2], NEG)
+            return jnp.maximum(tops[0], jnp.maximum(tops[1], tops[2]))
 
         top = lax.fori_loop(0, pairs, score_step, jnp.full((8, lanes), NEG, jnp.float32))
-        top = jnp.max(top, axis=0, keepdims=True)
-
-        def sum_step(pair, carry):
-            numer, total = carry
-            probs = jnp.exp2(score_ref[pair] - top)
-            upper = jnp.where(2 * pair + 1 < count, probs[key_block:], 0.0)
-            probs = jnp.concatenate([probs[:key_block], upper], axis=0).astype(jnp.bfloat16)
-            total = total + jnp.sum(
-                probs.astype(jnp.float32).reshape(2 * key_block // 8, 8, lanes), axis=0
+        top = jnp.max(top, axis=0, keepdims=True) * factor
+        sum_ref[...] = jnp.zeros_like(sum_ref)
+
+        def sum_step(pair, _):
+            shifts = [top, jnp.where(2 * pair + 1 < count, top, -NEG)]
+            probs = [
+                jnp.exp2(score_ref[pair, half * key_block : (half + 1) * key_block] * factor - shift)
+                for half, shift in enumerate(shifts)
+            ]
+            probs = jnp.concatenate([one.astype(jnp.bfloat16) for one in probs], axis=0)
+            both = [value_ref[:, pl.ds(start_of(2 * pair + half), key_block)] for half in range(2)]
+            sum_ref[...] += jnp.dot(
+                jnp.concatenate(both, axis=1), probs, preferred_element_type=jnp.float32
             )
-            both = jnp.concatenate([block_of(v_ref, 2 * pair), block_of(v_ref, 2 * pair + 1)], axis=0)
-            numer = numer + lax.dot_general(
-                both, probs, (((0,), (0,)), ((), ())), preferred_element_type=jnp.float32
-            )
-            return numer, total
-
-        numer, total = lax.fori_loop(
-            0,
-            pairs,
-            sum_step,
-            (jnp.zeros((HEAD_SIZE, lanes), jnp.float32), jnp.zeros((8, lanes), jnp.float32)),
-        )
+            return 0
+
+        lax.fori_loop(0, pairs, sum_step, 0)
+        numer = sum_ref[:HEAD_SIZE]
         top_ref[0, at : at + 1, :] = top
-        total_ref[0, at : at + 1, :] = jnp.sum(total, axis=0, keepdims=True)
+        total_ref[0, at : at + 1, :] = sum_ref[HEAD_SIZE : HEAD_SIZE + 1]
         for g in range(group):
             columns = slice(g * query_block, (g + 1) * query_block)
             out_columns = slice(g * HEAD_SIZE, (g + 1) * HEAD_SIZE)
@@ -121,6 +118,9 @@
         scratch_shapes=[
             pltpu.SMEM((key_blocks + 2,), jnp.int32),
             pltpu.VMEM(((key_blocks + 1) // 2, 2 * kdev // key_blocks, lanes), jnp.float32),
+            pltpu.VMEM((HEAD_SIZE, lanes), jnp.bfloat16),
+            pltpu.VMEM((HEAD_SIZE + ONES, kdev), jnp.bfloat16),
+            pltpu.VMEM((HEAD_SIZE + ONES, lanes), jnp.float32),
         ],
         compiler_params=pltpu.CompilerParams(vmem_limit_bytes=60 * 2**20),
         name="attend",
@@ -401,15 +401,18 @@
     return top, factors, total
 
 
-def combine_kernel(n, kept_ref, sent_ref, stat_ref, cols_ref, *scratch):
+def combine_kernel(n, kept_hbm, sent_ref, stat_ref, cols_ref, *scratch):
     numer_scratch, stat_scratch = scratch[:8], scratch[8:16]
-    piece_ref, swap_send, swap_recv, own_sem = scratch[16:]
+    piece_ref, swap_send, swap_recv, own_sem, kept_ref, kept_sem = scratch[16:]
+    keep = pltpu.make_async_copy(kept_hbm, kept_ref, kept_sem)
+    keep.start()
     me, plane, x, core = place(n)
     planes = n // (CORES * ROW)
     width = kept_ref.shape[-1]
     heads = width // HEAD_SIZE
     others = [lax.rem(me + step, n) for step in range(1, n)]
     greet(others)
+    keep.wait()
 
     def merge(one, two, out):
         top, factors, total = weigh([one[1][...], two[1][...]])
@@ -472,7 +475,8 @@
     cols = pl.pallas_call(
         functools.partial(combine_kernel, n),
         out_shape=jax.ShapeDtypeStruct((n, rows, width // n), jnp.bfloat16),
-        in_specs=[pl.BlockSpec(memory_space=pltpu.VMEM)] * 3,
+        in_specs=[pl.BlockSpec(memory_space=pl.ANY)] * 2
+        + [pl.BlockSpec(memory_space=pltpu.VMEM)],
         out_specs=pl.BlockSpec(memory_space=pltpu.VMEM),
         scratch_shapes=reduce_scratch(planes, rows, width, jnp.bfloat16)
         + reduce_scratch(planes, rows, STATS, jnp.float32)
@@ -481,9 +485,11 @@
             pltpu.SemaphoreType.DMA((n,)),
             pltpu.SemaphoreType.DMA((n,)),
             pltpu.SemaphoreType.DMA,
+            pltpu.VMEM((planes, ROW, rows, width), jnp.float32),
+            pltpu.SemaphoreType.DMA,
         ],
         compiler_params=pltpu.CompilerParams(
-            collective_id=1, has_side_effects=True, vmem_limit_bytes=40 * 2**20
+            collective_id=1, has_side_effects=True, vmem_limit_bytes=60 * 2**20
         ),
         name="combine",
     )(
@@ -497,10 +503,17 @@
 TILE = 512
 
 
-def project_kernel(n, cols_ref, weight_ref, out_ref, kept_ref, sent_ref, *scratch):
+def project_kernel(n, cols_ref, weight_hbm, out_ref, weight_ref, weight_sem, kept_ref, sent_ref, *scratch):
     _, plane, x, core = place(n)
     planes = n // (CORES * ROW)
     rows, width = out_ref.shape
+
+    def fetch(tile):
+        at = pl.ds(pl.multiple_of(tile * TILE, TILE), TILE)
+        return pltpu.make_async_copy(weight_hbm.at[:, at], weight_ref.at[:, at], weight_sem.at[tile])
+
+    for tile in range(width // TILE):
+        fetch(tile).start()
     greet(
         [index_of(lax.rem(plane + step, planes), x, core) for step in range(1, planes)]
         + [index_of(plane, 1 - x, core), index_of(plane, x, 1 - core)]
@@ -508,6 +521,7 @@
 
     def tile_step(tile, _):
         at = pl.ds(pl.multiple_of(tile * TILE, TILE), TILE)
+        fetch(tile).wait()
         product = jnp.dot(cols_ref[...], weight_ref[:, at], preferred_element_type=jnp.float32)
         product = product.reshape(planes, ROW, CORES, rows, TILE)
         kept_ref[:, :, :, at] = jnp.where(core == 0, product[:, :, 0], product[:, :, 1])
@@ -537,12 +551,16 @@
     return pl.pallas_call(
         functools.partial(project_kernel, n),
         out_shape=jax.ShapeDtypeStruct((rows, width), jnp.bfloat16),
-        in_specs=[pl.BlockSpec(memory_space=pltpu.VMEM)] * 2,
+        in_specs=[pl.BlockSpec(memory_space=pltpu.VMEM), pl.BlockSpec(memory_space=pl.ANY)],
         out_specs=pl.BlockSpec(memory_space=pltpu.VMEM),
-        scratch_shapes=[pltpu.VMEM((planes, ROW, rows, width), t) for t in (jnp.float32, jnp.bfloat16)]
+        scratch_shapes=[
+            pltpu.VMEM(weight.shape, weight.dtype),
+            pltpu.SemaphoreType.DMA((width // TILE,)),
+        ]
+        + [pltpu.VMEM((planes, ROW, rows, width), t) for t in (jnp.float32, jnp.bfloat16)]
         + reduce_scratch(planes, rows, width, jnp.bfloat16),
         compiler_params=pltpu.CompilerParams(
-            collective_id=2, has_side_effects=True, vmem_limit_bytes=40 * 2**20
+            collective_id=2, has_side_effects=True, vmem_limit_bytes=60 * 2**20
         ),
         name="project",
     )(cols, weight)

time: 131 us -> 134 us (1.023); the launches traced: 133 us -> 135 us
  Pallas kernels: 127 us -> 130 us
  local copies, waits for them, and re-layouts: 5.64 us -> 4.01 us
    pallas_call x1, Pallas kernels: 33.5 us -> 46.9 us  [combine(): pl.pallas_call(functools.partial(combine_kernel, n), out_shape=jax.ShapeD...]
    pallas_call x1, Pallas kernels: 37.1 us -> 25.1 us  [attend(): pl.pallas_call(functools.partial(attend_kernel, rows_each), grid=(heads_k...]
    unnamed x7 -> x1, local copies, waits for them, and re-layouts: 3.73 us -> 1.59 us
    pallas_call x1, Pallas kernels: 29.5 us -> 31.2 us  [project(): pl.pallas_call(functools.partial(project_kernel, n), out_shape=jax.ShapeD...]
where the time goes in v4:
time: 134 us; the launch traced here: 135 us
  Pallas kernels  130 us (97%)
  local copies, waits for them, and re-layouts  4.01 us (3%)
    pallas_call x1, Pallas kernels, combine(): pl.pallas_call(functools.partial(combine_kernel, n), out_shape=jax.ShapeD...  46.9 us
    pallas_call x1, Pallas kernels, project(): pl.pallas_call(functools.partial(project_kernel, n), out_shape=jax.ShapeD...  31.2 us
    pallas_call x1, Pallas kernels, gather_rows(): pl.pallas_call(functools.partial(gather_kernel, n), out_shape=jax.ShapeDt...  27.3 us
    pallas_call x1, Pallas kernels, attend(): pl.pallas_call(functools.partial(attend_kernel, rows_each), grid=(heads_k...  25.1 us

profile of v4, /device:TPU:0, one launch (start us, length us, event | category | flops | bytes accessed | tf_op | source)
XLA Modules:
  0.0 134.5 jit_solution(17941909410332584695)
XLA Ops:
  0.0 27.3 %gather_rows.1 = bf16[16,16,5120]{2,1,0:T(8,128)(2,1)} custom-call(bf16[16,5120]{1,0:T(8,128)(2,1)} %own_ref.1), custom_call_target="tpu_custom_call" | custom-call | tf_op jit(solution)/shard_map/gather_rows/pallas_call | solution.py:289
  27.3 25.1 %attend.1 = (f32[128,5120]{1,0:T(8,128)}, bf16[128,5120]{1,0:T(8,128)(2,1)}, f32[8,2,640]{2,1,0:T(2,128)}, f32[8,2,640]{2,1,0:T(2,128)}) custom-call(s32[8,2,12]{2,1,0:T(2,128)} %mask_ref.1, bf16[256,5120]{1,0:T(8,128)(2,1)} %bitcast.23, bf16[1536,1024]{1,0:T(8,128)(2,1)} %k_ref.1, bf16[1536,1024]{1,0:T(8,128)(2,1)} %v_ref.1), custom_call_target="tpu_custom_call" | custom-call | tf_op jit(solution)/shard_map/attend/pallas_call | solution.py:103
  52.4 0.8 copy.8
  53.3 0.8 copy.10
  54.1 0.8 copy.12
  54.9 46.9 %combine.1 = bf16[16,16,320]{2,1,0:T(8,128)(2,1)} custom-call(f32[4,2,16,5120]{3,2,1,0:T(8,128)} %bitcast.24, bf16[4,2,16,5120]{3,2,1,0:T(8,128)(2,1)} %bitcast.25, f32[4,2,2,16,128]{4,3,2,1,0:T(8,128)} %bitcast.27), custom_call_target="tpu_custom_call" | custom-call | tf_op jit(solution)/shard_map/combine/pallas_call | solution.py:475
  101.8 31.2 %project.1 = bf16[16,5120]{1,0:T(8,128)(2,1)} custom-call(bf16[256,320]{1,0:T(8,128)(2,1)} %bitcast.26, bf16[320,5120]{1,0:T(8,128)(2,1)} %weight_hbm.1), custom_call_target="tpu_custom_call" | custom-call | tf_op jit(solution)/shard_map/project/pallas_call | solution.py:551
  133.0 1.6 %copy.18 = bf16[16,5120]{1,0:T(8,128)(2,1)} copy(bf16[16,5120]{1,0:T(8,128)(2,1)} %project.1) | data formatting | bytes 327680
  (6 shorter events, 0.1 us)
